TPU v7x, 32 devices: a whole 2x2x4 slice. The times are simulated.
32 devices in a mesh: dp: 8 (over z, x), th: 2 (over core), tw: 2 (over y).
Axes of the slice: x: 2, y: 2, z: 4, core: 2. Of those that a mesh axis runs over, the one named last changes fastest.
Arguments:
- tokens: bfloat16 [16, 1536, 768], P('dp', ('th', 'tw')), may hold values from -6 to 6
- segment_ids: int32 [16, 1536], P('dp'), may hold values from 0 to 7, never falling along the last dimension, each value on 1 to 768 neighbouring positions
- norm1_gain: float32 [768], replicated, may hold values from 0.5 to 1.5
- norm1_shift: float32 [768], replicated, may hold values from -3 to 3
- w_qkv: bfloat16 [3, 768, 768], P(None, None, ('th', 'tw')), may hold values from -0.21875 to 0.21875
- b_qv: float32 [2, 768], P(None, ('th', 'tw')), may hold values from -3 to 3
- w_out: bfloat16 [768, 768], P(('th', 'tw')), may hold values from -0.875 to 0.875
- b_out: float32 [768], replicated, may hold values from -3 to 3
- norm2_gain: float32 [768], replicated, may hold values from 0.5 to 1.5
- norm2_shift: float32 [768], replicated, may hold values from -3 to 3
- w_up: bfloat16 [768, 3072], replicated, may hold values from -0.21875 to 0.21875
- b_up: float32 [3072], replicated, may hold values from -3 to 3
- w_down: bfloat16 [3072, 768], replicated, may hold values from -0.109375 to 0.109375
- b_down: float32 [768], replicated, may hold values from -3 to 3
- cotangent: bfloat16 [16, 1536, 768], P('dp', ('th', 'tw')), may hold values from -6 to 6
Outputs:
- block_out: bfloat16 [16, 1536, 768], P('dp', ('th', 'tw'))
- grad_tokens: bfloat16 [16, 1536, 768], P('dp', ('th', 'tw'))
- grad_norm1_gain: float32 [768], replicated
- grad_norm1_shift: float32 [768], replicated
- grad_w_qkv: float32 [3, 768, 768], P(None, None, ('th', 'tw'))
- grad_b_qv: float32 [2, 768], P(None, ('th', 'tw'))
- grad_w_out: float32 [768, 768], P(('th', 'tw'))
- grad_b_out: float32 [768], replicated
- grad_norm2_gain: float32 [768], replicated
- grad_norm2_shift: float32 [768], replicated
- grad_w_up: float32 [768, 3072], replicated
- grad_b_up: float32 [3072], replicated
- grad_w_down: float32 [3072, 768], replicated
- grad_b_down: float32 [768], replicated
Inputs may be any that keep to these rules, and one draw needn't show every extreme that they name: `segment_ids`: within each row the ids never fall, and one image holds 1 to 768 tokens.
All inputs are finite; a program needn't handle non-finite values.
Results may differ from a plain program's by a relative error of at most 0.015.
Values may be sent and summed in bfloat16 or wider, within the bound.
A program may use at most 192 MiB of HBM per device.

v0:
```python
import jax
import jax.numpy as jnp
from jax import lax
from jax.sharding import PartitionSpec as P

HD = 64
EPSILON = 1e-06


def layer_norm(field, norm_gain, norm_shift):
    average = jnp.mean(field, axis=-1, keepdims=True)
    centred = field - average
    spread = jnp.mean(centred * centred, axis=-1, keepdims=True)
    return centred * lax.rsqrt(spread + EPSILON) * norm_gain + norm_shift


def gelu_exact(field):
    return jax.nn.gelu(field, approximate=False)


def masked_scores(query_block, key_rows, row_seg, offset, block_rows):
    score_scale = query_block.shape[-1] ** (-0.5)
    same_image = row_seg[offset : offset + block_rows, None] == row_seg[None, :]
    scores = (
        jnp.einsum("qhe,khe->hqk", query_block, key_rows, preferred_element_type=jnp.float32)
        * score_scale
    )
    return jnp.where(same_image[None], scores, -1000000000.0)


def row_forward(row_items):
    row_qkv, row_seg = row_items
    length = row_qkv.shape[1]
    head_count = row_qkv.shape[2] // HD
    key_rows = row_qkv[1].reshape(length, head_count, HD)
    value_rows = row_qkv[2].reshape(length, head_count, HD)
    block_rows = min(512, length)
    head_outs = []
    log_totals = []
    for offset in range(0, length, block_rows):
        query_block = row_qkv[0, offset : offset + block_rows].reshape(block_rows, head_count, HD)
        scores = masked_scores(query_block, key_rows, row_seg, offset, block_rows)
        row_peak = jnp.max(scores, axis=-1, keepdims=True)
        exponent = jnp.exp(scores - row_peak)
        denominator = jnp.sum(exponent, axis=-1, keepdims=True)
        weights_low = (exponent / denominator).astype(jnp.bfloat16)
        head_out = jnp.einsum(
            "hqk,khe->qhe", weights_low, value_rows, preferred_element_type=jnp.float32
        )
        head_outs.append(head_out.reshape(block_rows, head_count * HD).astype(jnp.bfloat16))
        log_totals.append((row_peak + jnp.log(denominator))[..., 0])
    return (jnp.concatenate(head_outs, 0), jnp.concatenate(log_totals, 1))


def row_backward(row_items):
    row_qkv, row_grad, row_total, row_seg = row_items
    length = row_qkv.shape[1]
    head_count = row_qkv.shape[2] // HD
    score_scale = HD ** (-0.5)
    key_rows = row_qkv[1].reshape(length, head_count, HD)
    value_rows = row_qkv[2].reshape(length, head_count, HD)
    block_rows = min(512, length)
    key_grad = jnp.zeros((length, head_count, HD), jnp.float32)
    value_grad = jnp.zeros((length, head_count, HD), jnp.float32)
    query_grads = []
    for offset in range(0, length, block_rows):
        query_block = row_qkv[0, offset : offset + block_rows].reshape(block_rows, head_count, HD)
        upstream = row_grad[offset : offset + block_rows].reshape(block_rows, head_count, HD)
        scores = masked_scores(query_block, key_rows, row_seg, offset, block_rows)
        probability = jnp.exp(scores - row_total[:, offset : offset + block_rows, None])
        value_grad = value_grad + jnp.einsum(
            "hqk,qhe->khe",
            probability.astype(jnp.bfloat16),
            upstream,
            preferred_element_type=jnp.float32,
        )
        prob_grad = jnp.einsum(
            "qhe,khe->hqk", upstream, value_rows, preferred_element_type=jnp.float32
        )
        row_inner = jnp.sum(probability * prob_grad, axis=-1, keepdims=True)
        score_grad = (probability * (prob_grad - row_inner)).astype(jnp.bfloat16) * score_scale
        query_grad = jnp.einsum(
            "hqk,khe->qhe", score_grad, key_rows, preferred_element_type=jnp.float32
        )
        query_grads.append(query_grad.reshape(block_rows, head_count * HD))
        key_grad = key_grad + jnp.einsum(
            "hqk,qhe->khe", score_grad, query_block, preferred_element_type=jnp.float32
        )
    stacked = jnp.stack(
        [
            jnp.concatenate(query_grads, 0),
            key_grad.reshape(length, head_count * HD),
            value_grad.reshape(length, head_count * HD),
        ]
    )
    return stacked.astype(jnp.bfloat16)


def body(
    tokens,
    segment_ids,
    norm1_gain,
    norm1_shift,
    w_qkv,
    b_qv,
    w_out,
    b_out,
    norm2_gain,
    norm2_shift,
    w_up,
    b_up,
    w_down,
    b_down,
    cotangent,
):
    inputs = tokens.astype(jnp.float32)
    normed_one, norm_one_back = jax.vjp(layer_norm, inputs, norm1_gain, norm1_shift)
    normed_low = normed_one.astype(jnp.bfloat16)
    gathered = lax.all_gather(normed_low, ("th", "tw"), axis=1, tiled=True)
    bias_rows = jnp.stack([b_qv[0], jnp.zeros_like(b_qv[0]), b_qv[1]])
    projected = jnp.einsum("rld,cde->rcle", gathered, w_qkv, preferred_element_type=jnp.float32)
    projected_low = (projected + bias_rows[None, :, None, :]).astype(jnp.bfloat16)
    heads_out, totals = lax.map(row_forward, (projected_low, segment_ids))
    partial_out = jnp.einsum("rle,ed->rld", heads_out, w_out, preferred_element_type=jnp.float32)
    branch = (
        lax.psum_scatter(
            partial_out.astype(jnp.bfloat16), ("th", "tw"), scatter_dimension=1, tiled=True
        ).astype(jnp.float32)
        + b_out
    )
    middle = inputs + branch
    normed_two, norm_two_back = jax.vjp(layer_norm, middle, norm2_gain, norm2_shift)
    second_low = normed_two.astype(jnp.bfloat16)
    hidden_pre = (
        jnp.einsum("rld,df->rlf", second_low, w_up, preferred_element_type=jnp.float32) + b_up
    )
    activated, gelu_back = jax.vjp(gelu_exact, hidden_pre)
    active_low = activated.astype(jnp.bfloat16)
    block_out = middle + (
        jnp.einsum("rlf,fd->rld", active_low, w_down, preferred_element_type=jnp.float32) + b_down
    )
    upstream = cotangent.astype(jnp.float32)
    grad_w_down = jnp.einsum(
        "rlf,rld->fd", active_low, cotangent, preferred_element_type=jnp.float32
    )
    grad_b_down = jnp.sum(upstream, axis=(0, 1))
    grad_active = jnp.einsum("rld,fd->rlf", cotangent, w_down, preferred_element_type=jnp.float32)
    grad_hidden = gelu_back(grad_active)[0].astype(jnp.bfloat16)
    grad_w_up = jnp.einsum(
        "rld,rlf->df", second_low, grad_hidden, preferred_element_type=jnp.float32
    )
    grad_b_up = jnp.sum(grad_hidden.astype(jnp.float32), axis=(0, 1))
    grad_normed_two = jnp.einsum(
        "rlf,df->rld", grad_hidden, w_up, preferred_element_type=jnp.float32
    )
    grad_mid_norm, grad_gain_two, grad_shift_two = norm_two_back(grad_normed_two)
    grad_middle = upstream + grad_mid_norm
    grad_branch = grad_middle.astype(jnp.bfloat16)
    grad_b_out = jnp.sum(grad_branch.astype(jnp.float32), axis=(0, 1))
    grad_whole = lax.all_gather(grad_branch, ("th", "tw"), axis=1, tiled=True)
    grad_heads = jnp.einsum(
        "rld,ed->rle", grad_whole, w_out, preferred_element_type=jnp.float32
    ).astype(jnp.bfloat16)
    grad_w_out = jnp.einsum(
        "rle,rld->ed", heads_out, grad_whole, preferred_element_type=jnp.float32
    )
    grad_qkv = lax.map(row_backward, (projected_low, grad_heads, totals, segment_ids))
    grad_w_qkv = jnp.einsum("rld,rcle->cde", gathered, grad_qkv, preferred_element_type=jnp.float32)
    grad_b_qv = jnp.sum(grad_qkv[:, 0::2].astype(jnp.float32), axis=(0, 2))
    grad_normed = jnp.einsum("rcle,cde->rld", grad_qkv, w_qkv, preferred_element_type=jnp.float32)
    grad_tile = lax.psum_scatter(
        grad_normed.astype(jnp.bfloat16), ("th", "tw"), scatter_dimension=1, tiled=True
    ).astype(jnp.float32)
    grad_inputs, grad_gain_one, grad_shift_one = norm_one_back(grad_tile)
    grad_tokens = (grad_middle + grad_inputs).astype(jnp.bfloat16)
    head_sums = (
        lax.psum(grad_w_qkv.astype(jnp.bfloat16), "dp").astype(jnp.float32),
        lax.psum(grad_b_qv.astype(jnp.bfloat16), "dp").astype(jnp.float32),
        lax.psum(grad_w_out.astype(jnp.bfloat16), "dp").astype(jnp.float32),
    )
    shared = lax.psum(
        (
            grad_gain_one,
            grad_shift_one,
            grad_b_out,
            grad_gain_two,
            grad_shift_two,
            grad_w_up,
            grad_b_up,
            grad_w_down,
            grad_b_down,
        ),
        ("dp", "th", "tw"),
    )
    return (
        block_out.astype(jnp.bfloat16),
        grad_tokens,
        shared[0],
        shared[1],
        head_sums[0],
        head_sums[1],
        head_sums[2],
        shared[2],
        shared[3],
        shared[4],
        shared[5],
        shared[6],
        shared[7],
        shared[8],
    )


def solution(mesh):
    return jax.shard_map(
        body,
        mesh=mesh,
        in_specs=(
            P("dp", ("th", "tw"), None),
            P("dp", None),
            P(),
            P(),
            P(None, None, ("th", "tw")),
            P(None, ("th", "tw")),
            P(("th", "tw"), None),
            P(),
            P(),
            P(),
            P(),
            P(),
            P(),
            P(),
            P("dp", ("th", "tw"), None),
        ),
        out_specs=(
            P("dp", ("th", "tw"), None),
            P("dp", ("th", "tw"), None),
            P(),
            P(),
            P(None, None, ("th", "tw")),
            P(None, ("th", "tw")),
            P(("th", "tw"), None),
            P(),
            P(),
            P(),
            P(),
            P(),
            P(),
            P(),
        ),
        check_vma=False,
    )
```

profile of v0, /device:TPU:0, one launch (start us, length us, event | category | flops | bytes accessed | tf_op | source)
XLA Modules:
  0.0 1006.1 jit_solution(13144696597506998621)
XLA Ops:
  11.7 2.8 fusion.160
  14.8 40.1 %all-gather.3.cloned.1.call-done = bf16[2,1536,768]{2,1,0:T(8,128)(2,1)} async-done(((bf16[2,384,768]{2,1,0:T(8,128)(2,1)}), bf16[2,1536,768]{2,1,0:T(8,128)(2,1)}) %all-gather.3.cloned.1.call-update) | async-done | bytes 4718608 | tf_op jit(solution)/shard_map/all_gather | solution.py:119
  54.9 6.7 fusion.154
  61.6 59.3 %while.22 = (s32[]{:T(128)}, bf16[2,1536,192]{1,2,0:T(8,128)(2,1)S(1)}, f32[2,3,1536]{2,1,0:T(4,128)S(1)}, bf16[2,3,1536,192]{2,3,1,0:T(8,128)(2,1)}, s32[2,1536...) while((s32[]{:T(128)}, bf16[2,1536,192]{1,2,0:T(8,128)(2,1)S(1)}, ...), condition=%wide.region_9.10_spmd, body=%wide.region_2.9_spmd.sunk | while | flops 1901302272 | bytes 107581632 | solution.py:123
  68.4 2.8 fusion.320
  71.2 3.5 fusion.321
  78.7 5.2 fusion.324
  83.9 3.5 fusion.326
  87.4 3.5 fusion.325
  97.6 2.8 fusion.320
  100.4 3.5 fusion.321
  108.0 5.2 fusion.324
  113.1 3.5 fusion.326
  116.7 3.5 fusion.325
  120.9 4.9 convolution_convert_fusion
  125.9 47.9 %reduce-scatter.3.cloned.1.call-done = bf16[2,384,768]{2,1,0:T(8,128)(2,1)} async-done(((bf16[2,1536,768]{2,1,0:T(8,128)(2,1)}), bf16[2,384,768]{2,1,0:T(8,128)(2,1)}) %reduce-scatter.3.cloned.1.call-update) | async-done | bytes 1179664 | tf_op jit(solution)/shard_map/reduce_scatter | solution.py:126
  177.7 9.2 fusion.165
  186.9 23.4 %multiply_convert_fusion.3 = (bf16[2,384,3072]{2,1,0:T(8,128)(2,1)}, f32[2,384,3072]{2,1,0:T(8,128)}) fusion(f32[2,384,3072]{2,1,0:T(8,128)S(1)} %get-tuple-element.164, f32[3072]{0:T(1024)S(1)} %copy-done.45, u8[384,3072]{1,0:T(8,128)(4,1)S(1)} %get-tuple-element.78, u8[384,3072]{1,0:T(8,128)(4,1)S(1)} %get-tuple-element.77), kind=kLoop, calls=%fused_computation.126 | loop fusion | flops 167510016 | bytes 25964544 | tf_op jit(solution)/shard_map/convert_element_type | solution.py:138
  210.2 12.5 %convert_reduce_fusion = (f32[3072]{0:T(1024)}, bf16[2,384,3072]{2,1,0:T(8,128)(2,1)}) fusion(f32[2,384,3072]{2,1,0:T(8,128)} %get-tuple-element.123, bf16[2,384,768]{2,1,0:T(8,128)(2,1)S(1)} %copy-done.15, bf16[3072,768]{1,0:T(8,128)(2,1)} %param.31, f32[2,384,3072]{2,1,0:T(8,128)S(1)} %get-tuple-element.164, f32[3072]{0:T(1024)S(1)} %copy-done.45), kind=kOutput, calls=%fused_computation.124 | convolution fusion | flops 3663983616 | bytes 29515776 | tf_op jit(solution)/shard_map/rld,fd->rlf/dot_general | solution.py:147
  222.8 8.1 fusion.185
  232.9 2.7 convert_reduce_fusion.4
  235.7 37.6 %all-gather.5.cloned.1.call-done = bf16[2,1536,768]{2,1,0:T(8,128)(2,1)} async-done(((bf16[2,384,768]{2,1,0:T(8,128)(2,1)}), bf16[2,1536,768]{2,1,0:T(8,128)(2,1)}) %all-gather.5.cloned.1.call-update) | async-done | bytes 4718608 | tf_op jit(solution)/shard_map/all_gather | solution.py:160
  273.3 5.0 convolution_convert_fusion.1
  278.3 254.2 %while.23 = (s32[]{:T(128)}, bf16[2,3,1536,192]{2,3,1,0:T(8,128)(2,1)}, bf16[2,3,1536,192]{2,3,1,0:T(8,128)(2,1)}, s32[2,1536]{1,0:T(2,128)S(1)}, f32[2,3,1536]{...) while((s32[]{:T(128)}, ...), condition=%wide.region_19.20_spmd, body=%wide.region_15.19_spmd.sunk | while | flops 4682926080 | bytes 364640672 | solution.py:167
  283.2 2.5 subtract_exponential_fusion.9
  286.7 2.6 copy-done.2
  289.3 2.5 subtract_exponential_fusion.11
  294.2 4.3 copy-done.3
  300.4 5.2 fusion.371
  305.6 15.2 %fusion.377 = bf16[3,64,512]{2,1,0:T(8,128)(2,1)} fusion(bf16[1536,3,64]{0,2,1:T(8,128)(2,1)S(1)} %bitcast.312, f32[3,512,1536]{2,1,0:T(8,128)} %copy-done.4, f32[3,512,1536]{2,1,0:T(8,128)} %fusion.371), kind=kOutput, calls=%fused_computation.94.clone.1 | convolution fusion | flops 320965632 | bytes 19660800 | tf_op jit(solution)/shard_map/while/body/eval_jaxpr/hqk,khe->qhe/dot_general | solution.py:82
  320.8 15.3 %fusion.372 = f32[3,64,1536]{2,1,0:T(8,128)} fusion(bf16[512,3,64]{0,2,1:T(8,128)(2,1)} %bitcast.323, f32[3,512,1536]{2,1,0:T(8,128)} %copy-done.4, f32[3,512,1536]{2,1,0:T(8,128)} %fusion.371), kind=kOutput, calls=%fused_computation.63.clone.1 | convolution fusion | flops 320867328 | bytes 20250624 | tf_op jit(solution)/shard_map/while/body/eval_jaxpr/hqk,qhe->khe/dot_general | solution.py:86
  336.1 5.2 fusion.375
  341.3 14.4 %fusion.379 = bf16[3,64,512]{2,1,0:T(8,128)(2,1)S(1)} fusion(bf16[1536,3,64]{0,2,1:T(8,128)(2,1)S(1)} %bitcast.313, f32[3,512,1536]{2,1,0:T(8,128)} %copy-done.3, f32[3,512,1536]{2,1,0:T(8,128)} %fusion.375), kind=kOutput, calls=%fused_computation.92.clone.1 | convolution fusion | flops 320965632 | bytes 19660800 | tf_op jit(solution)/shard_map/while/body/eval_jaxpr/hqk,khe->qhe/dot_general | solution.py:82
  355.6 5.2 fusion.373
  360.8 15.0 %fusion.378 = bf16[3,64,512]{2,1,0:T(8,128)(2,1)} fusion(bf16[1536,3,64]{0,2,1:T(8,128)(2,1)S(1)} %bitcast.314, f32[3,512,1536]{2,1,0:T(8,128)} %copy-done.2, f32[3,512,1536]{2,1,0:T(8,128)} %fusion.373), kind=kOutput, calls=%fused_computation.93.clone.1 | convolution fusion | flops 320965632 | bytes 19660800 | tf_op jit(solution)/shard_map/while/body/eval_jaxpr/hqk,khe->qhe/dot_general | solution.py:82
  375.8 14.1 %fusion.374 = f32[3,64,1536]{2,1,0:T(8,128)} fusion(bf16[512,3,64]{0,2,1:T(8,128)(2,1)S(1)} %bitcast.321, f32[3,512,1536]{2,1,0:T(8,128)} %copy-done.2, f32[3,512,1536]{2,1,0:T(8,128)} %fusion.373), kind=kOutput, calls=%fused_computation.67.clone.1 | convolution fusion | flops 320867328 | bytes 20250624 | tf_op jit(solution)/shard_map/while/body/eval_jaxpr/hqk,qhe->khe/dot_general | solution.py:86
  389.9 14.1 %fusion.376 = bf16[3,64,1536]{2,1,0:T(8,128)(2,1)S(1)} fusion(f32[3,64,1536]{2,1,0:T(8,128)} %fusion.372, f32[3,64,1536]{2,1,0:T(8,128)} %fusion.374, bf16[512,3,64]{0,2,1:T(8,128)(2,1)S(1)} %bitcast.319, f32[3,512,1536]{2,1,0:T(8,128)} %copy-done.3, f32[3,512,1536]{2,1,0:T(8,128)} %fusion.375), kind=kOutput, calls=%fused_computation.79.clone.1 | convolution fusion | flops 321752064 | bytes 22020096 | tf_op jit(solution)/shard_map/while/body/eval_jaxpr/hqk,qhe->khe/dot_general | solution.py:86
  413.5 2.6 copy-done.2
  421.0 4.3 copy-done.3
  427.2 5.2 fusion.371
  432.4 15.2 %fusion.377 = bf16[3,64,512]{2,1,0:T(8,128)(2,1)} fusion(bf16[1536,3,64]{0,2,1:T(8,128)(2,1)S(1)} %bitcast.312, f32[3,512,1536]{2,1,0:T(8,128)} %copy-done.4, f32[3,512,1536]{2,1,0:T(8,128)} %fusion.371), kind=kOutput, calls=%fused_computation.94.clone.1 | convolution fusion | flops 320965632 | bytes 19660800 | tf_op jit(solution)/shard_map/while/body/eval_jaxpr/hqk,khe->qhe/dot_general | solution.py:82
  447.6 15.3 %fusion.372 = f32[3,64,1536]{2,1,0:T(8,128)} fusion(bf16[512,3,64]{0,2,1:T(8,128)(2,1)} %bitcast.323, f32[3,512,1536]{2,1,0:T(8,128)} %copy-done.4, f32[3,512,1536]{2,1,0:T(8,128)} %fusion.371), kind=kOutput, calls=%fused_computation.63.clone.1 | convolution fusion | flops 320867328 | bytes 20250624 | tf_op jit(solution)/shard_map/while/body/eval_jaxpr/hqk,qhe->khe/dot_general | solution.py:86
  462.9 5.2 fusion.375
  468.1 14.4 %fusion.379 = bf16[3,64,512]{2,1,0:T(8,128)(2,1)S(1)} fusion(bf16[1536,3,64]{0,2,1:T(8,128)(2,1)S(1)} %bitcast.313, f32[3,512,1536]{2,1,0:T(8,128)} %copy-done.3, f32[3,512,1536]{2,1,0:T(8,128)} %fusion.375), kind=kOutput, calls=%fused_computation.92.clone.1 | convolution fusion | flops 320965632 | bytes 19660800 | tf_op jit(solution)/shard_map/while/body/eval_jaxpr/hqk,khe->qhe/dot_general | solution.py:82
  482.5 5.2 fusion.373
  487.6 15.0 %fusion.378 = bf16[3,64,512]{2,1,0:T(8,128)(2,1)} fusion(bf16[1536,3,64]{0,2,1:T(8,128)(2,1)S(1)} %bitcast.314, f32[3,512,1536]{2,1,0:T(8,128)} %copy-done.2, f32[3,512,1536]{2,1,0:T(8,128)} %fusion.373), kind=kOutput, calls=%fused_computation.93.clone.1 | convolution fusion | flops 320965632 | bytes 19660800 | tf_op jit(solution)/shard_map/while/body/eval_jaxpr/hqk,khe->qhe/dot_general | solution.py:82
  502.6 14.1 %fusion.374 = f32[3,64,1536]{2,1,0:T(8,128)} fusion(bf16[512,3,64]{0,2,1:T(8,128)(2,1)S(1)} %bitcast.321, f32[3,512,1536]{2,1,0:T(8,128)} %copy-done.2, f32[3,512,1536]{2,1,0:T(8,128)} %fusion.373), kind=kOutput, calls=%fused_computation.67.clone.1 | convolution fusion | flops 320867328 | bytes 20250624 | tf_op jit(solution)/shard_map/while/body/eval_jaxpr/hqk,qhe->khe/dot_general | solution.py:86
  516.8 14.1 %fusion.376 = bf16[3,64,1536]{2,1,0:T(8,128)(2,1)S(1)} fusion(f32[3,64,1536]{2,1,0:T(8,128)} %fusion.372, f32[3,64,1536]{2,1,0:T(8,128)} %fusion.374, bf16[512,3,64]{0,2,1:T(8,128)(2,1)S(1)} %bitcast.319, f32[3,512,1536]{2,1,0:T(8,128)} %copy-done.3, f32[3,512,1536]{2,1,0:T(8,128)} %fusion.375), kind=kOutput, calls=%fused_computation.79.clone.1 | convolution fusion | flops 321752064 | bytes 22020096 | tf_op jit(solution)/shard_map/while/body/eval_jaxpr/hqk,qhe->khe/dot_general | solution.py:86
  532.5 4.6 fusion.177
  537.2 6.2 fusion.174
  543.4 7.7 bitcast_convert_fusion
  551.2 10.5 %convolution_bitcast_fusion = f32[3072,768]{1,0:T(8,128)} fusion(bf16[2,384,3072]{2,1,0:T(8,128)(2,1)} %get-tuple-element.122, bf16[2,384,768]{2,1,0:T(8,128)(2,1)} %param.33), kind=kOutput, calls=%fused_computation.140 | convolution fusion | flops 3623878656 | bytes 15335424 | tf_op jit(solution)/shard_map/rlf,rld->fd/dot_general | solution.py:143
  561.7 9.2 convolution_bitcast_fusion.1
  571.7 8.8 add_convert_fusion.3
  580.9 21.5 %psum.87 = bf16[2,192]{1,0:T(2,128)(2,1)S(1)} all-reduce(bf16[2,192]{1,0:T(2,128)(2,1)S(1)} %slice_reduce_fusion), channel_id=1, replica_groups=mesh['dp'=8,'th'=2,'tw'=2] {'dp'}, use_global_device_ids=true, to_apply=%region_29.30 | all-reduce | flops 384 | bytes 1536 | tf_op jit(solution)/shard_map/psum | solution.py:178
  603.0 20.8 %all-reduce.8.cloned.1.call-done = (bf16[3,768,192]{1,2,0:T(8,128)(2,1)}, bf16[192,768]{1,0:T(8,128)(2,1)}) async-done(((bf16[3,768,192]{1,2,0:T(8,128)(2,1)}, bf16[192,768]{1,0:T(8,128)(2,1)}), (bf16[3,768,192]{1,2,0:T(8,128)(2,1)}, bf16[192,768]{1,0:T(8,128)(2,1)})) %all-reduce.8.cloned.1.call-update) | async-done | bytes 1179664 | tf_op jit(solution)/shard_map/psum | solution.py:177
  625.6 2.5 convert_element_type.154
  628.1 45.2 %reduce-scatter.5.cloned.1.call-done = bf16[2,384,768]{2,1,0:T(8,128)(2,1)} async-done(((bf16[2,1536,768]{2,1,0:T(8,128)(2,1)}), bf16[2,384,768]{2,1,0:T(8,128)(2,1)}) %reduce-scatter.5.cloned.1.call-update) | async-done | bytes 1179664 | tf_op jit(solution)/shard_map/reduce_scatter | solution.py:171
  675.6 2.7 fusion.163
  678.4 3.0 convert_reduce_fusion.3
  681.4 42.5 %all-reduce = (f32[768]{0:T(1024)}, f32[768]{0:T(1024)}, f32[768]{0:T(1024)}, f32[768]{0:T(1024)}, f32[768]{0:T(1024)}, /*index=5*/f32[3072]{0:T(1024)}, f32[768]{0:T(1024)}) all-reduce(f32[768]{0:T(1024)S(1)} %get-tuple-element.81, f32[768]{0:T(1024)S(1)} %get-tuple-element.85, ...), channel_id=1, replica_groups=mesh['dp'=8,'th'=2,'tw'=2] {'dp','th','tw'}, use_global_device_ids=true, to_apply=%region_24.25 | all-reduce | flops 7680 | bytes 61440 | tf_op jit(solution)/shard_map/psum | solution.py:181
  724.0 262.5 %all-reduce.6.cloned.1.call-done = (f32[768,3072]{1,0:T(8,128)}, f32[3072,768]{1,0:T(8,128)}) async-done(((f32[768,3072]{1,0:T(8,128)}, f32[3072,768]{1,0:T(8,128)}), (f32[768,3072]{1,0:T(8,128)}, f32[3072,768]{1,0:T(8,128)})) %all-reduce.6.cloned.1.call-update) | async-done | bytes 18874384 | tf_op jit(solution)/shard_map/psum | solution.py:181
  986.5 8.8 copy.59
  995.2 3.7 copy.60
  (212 shorter events, 65.0 us)
Async XLA Ops:
  7.2 47.7 %copy-start = (bf16[3,768,192]{1,2,0:T(8,128)(2,1)S(1)}, bf16[3,768,192]{1,2,0:T(8,128)(2,1)}, u32[]{:S(2)}) copy-start(bf16[3,768,192]{1,2,0:T(8,128)(2,1)} %param.23) | copy-start | bytes 2654212
  7.2 7.5 copy-start.48
  7.2 47.7 %all-gather.3.cloned.1.call-start = ((), (), s32[]{:S(2)}) async-start(), calls=%async_computation.2 | async-start | bytes 5898240 | tf_op jit(solution)/shard_map/all_gather | solution.py:119
  8.8 2.3 copy-start.32
  14.6 159.3 %reduce-scatter.3.cloned.1.call-start = ((), (), s32[]{:S(2)}) async-start(), calls=%async_computation.3 | async-start | bytes 5898240 | tf_op jit(solution)/shard_map/reduce_scatter | solution.py:126
  14.8 46.8 %copy-start.20 = (s32[2,1536]{1,0:T(2,128)S(1)}, s32[2,1536]{1,0:T(2,128)}, u32[]{:S(2)}) copy-start(s32[2,1536]{1,0:T(2,128)} %param.20) | copy-start | bytes 36868
  120.8 5.0 copy-start.17
  120.9 53.0 %copy-start.5 = (bf16[2,384,768]{2,1,0:T(8,128)(2,1)S(1)}, bf16[2,384,768]{2,1,0:T(8,128)(2,1)}, u32[]{:S(2)}) copy-start(bf16[2,384,768]{2,1,0:T(8,128)(2,1)} %param.19) | copy-start | bytes 3538948
  120.9 53.0 %copy-start.21 = (f32[768]{0:T(1024)S(1)}, f32[768]{0:T(1024)}, u32[]{:S(2)}) copy-start(f32[768]{0:T(1024)} %param.26) | copy-start | bytes 9220
  125.8 51.8 %copy-start.25 = (f32[768]{0:T(1024)S(1)}, f32[768]{0:T(1024)}, u32[]{:S(2)}) copy-start(f32[768]{0:T(1024)} %param.27) | copy-start | bytes 9220
  125.8 51.8 %copy-start.30 = (f32[768]{0:T(1024)S(1)}, f32[768]{0:T(1024)}, u32[]{:S(2)}) copy-start(f32[768]{0:T(1024)} %param.28) | copy-start | bytes 9220
  125.8 51.8 %copy-start.45 = (f32[3072]{0:T(1024)S(1)}, f32[3072]{0:T(1024)}, u32[]{:S(2)}) copy-start(f32[3072]{0:T(1024)} %param.30) | copy-start | bytes 36868
  125.8 147.5 %all-gather.5.cloned.1.call-start = ((), (), s32[]{:S(2)}) async-start(), calls=%async_computation.4 | async-start | bytes 5898240 | tf_op jit(solution)/shard_map/all_gather | solution.py:160
  173.8 3.8 copy-start.7
  175.7 57.2 %copy-start.23 = (f32[2,384]{1,0:T(2,128)}, f32[2,384]{1,0:T(2,128)S(1)}, u32[]{:S(2)}) copy-start(f32[2,384]{1,0:T(2,128)S(1)} %broadcast_multiply_fusion) | copy-start | bytes 9220
  177.7 55.3 %copy-start.27 = (f32[2,384]{1,0:T(2,128)}, f32[2,384]{1,0:T(2,128)S(1)}, u32[]{:S(2)}) copy-start(f32[2,384]{1,0:T(2,128)S(1)} %fusion.183) | copy-start | bytes 9220
  186.8 23.4 %copy-start.15 = (bf16[2,384,768]{2,1,0:T(8,128)(2,1)S(1)}, bf16[2,384,768]{2,1,0:T(8,128)(2,1)}, u32[]{:S(2)}) copy-start(bf16[2,384,768]{2,1,0:T(8,128)(2,1)} %param.33) | copy-start | bytes 3538948
  230.9 4.8 copy-start.9
  230.9 4.8 copy-start.35
  232.9 40.4 %copy-start.29 = (bf16[192,768]{1,0:T(8,128)(2,1)S(1)}, bf16[192,768]{1,0:T(8,128)(2,1)}, u32[]{:S(2)}) copy-start(bf16[192,768]{1,0:T(8,128)(2,1)} %param.25) | copy-start | bytes 884740
  232.9 45.4 %copy-start.39 = (f32[2,384]{1,0:T(2,128)}, f32[2,384]{1,0:T(2,128)S(1)}, u32[]{:S(2)}) copy-start(f32[2,384]{1,0:T(2,128)S(1)} %negate_multiply_fusion.2) | copy-start | bytes 9220
  235.7 388.1 %all-reduce.8.cloned.1.call-start = ((), (), s32[]{:S(2)}) async-start(), calls=%async_computation.7 | async-start | bytes 2359296 | tf_op jit(solution)/shard_map/psum | solution.py:177
  278.7 2.8 copy-start.1
  281.7 4.9 copy-start.12
  285.6 3.6 copy-start.2
  291.7 7.7 copy-start.4
  294.2 4.3 copy-start.3
  389.9 14.2 %copy-start.13 = (bf16[3,64,512]{2,1,0:T(8,128)(2,1)S(1)}, bf16[3,64,512]{2,1,0:T(8,128)(2,1)}, u32[]{:S(2)}) copy-start(bf16[3,64,512]{2,1,0:T(8,128)(2,1)} %fusion.377) | copy-start | bytes 589828 | tf_op jit(solution)/shard_map/while
  389.9 14.2 %copy-start.14 = (bf16[3,64,512]{2,1,0:T(8,128)(2,1)S(1)}, bf16[3,64,512]{2,1,0:T(8,128)(2,1)}, u32[]{:S(2)}) copy-start(bf16[3,64,512]{2,1,0:T(8,128)(2,1)} %fusion.378) | copy-start | bytes 589828 | tf_op jit(solution)/shard_map/while
  405.6 2.8 copy-start.1
  408.6 4.9 copy-start.12
  412.5 3.6 copy-start.2
  418.6 7.7 copy-start.4
  421.0 4.3 copy-start.3
  516.7 14.2 %copy-start.13 = (bf16[3,64,512]{2,1,0:T(8,128)(2,1)S(1)}, bf16[3,64,512]{2,1,0:T(8,128)(2,1)}, u32[]{:S(2)}) copy-start(bf16[3,64,512]{2,1,0:T(8,128)(2,1)} %fusion.377) | copy-start | bytes 589828 | tf_op jit(solution)/shard_map/while
  516.8 14.2 %copy-start.14 = (bf16[3,64,512]{2,1,0:T(8,128)(2,1)S(1)}, bf16[3,64,512]{2,1,0:T(8,128)(2,1)}, u32[]{:S(2)}) copy-start(bf16[3,64,512]{2,1,0:T(8,128)(2,1)} %fusion.378) | copy-start | bytes 589828 | tf_op jit(solution)/shard_map/while
  532.5 4.7 copy-start.18
  543.3 130.0 %reduce-scatter.5.cloned.1.call-start = ((), (), s32[]{:S(2)}) async-start(), calls=%async_computation.5 | async-start | bytes 5898240 | tf_op jit(solution)/shard_map/reduce_scatter | solution.py:171
  551.1 435.4 %all-reduce.6.cloned.1.call-start = ((), (), s32[]{:S(2)}) async-start(), calls=%async_computation.6 | async-start | bytes 37748736 | tf_op jit(solution)/shard_map/psum | solution.py:181
  551.1 10.6 %copy-start.6 = (bf16[2,384,768]{2,1,0:T(8,128)(2,1)S(1)}, bf16[2,384,768]{2,1,0:T(8,128)(2,1)}, u32[]{:S(2)}) copy-start(bf16[2,384,768]{2,1,0:T(8,128)(2,1)} %param.19) | copy-start | bytes 3538948
  551.1 10.6 %copy-start.8 = (bf16[2,384,768]{2,1,0:T(8,128)(2,1)S(1)}, bf16[2,384,768]{2,1,0:T(8,128)(2,1)}, u32[]{:S(2)}) copy-start(bf16[2,384,768]{2,1,0:T(8,128)(2,1)} %reduce-scatter.3.cloned.1.call-done) | copy-start | bytes 3538948
  551.2 10.5 %copy-start.22 = (f32[768]{0:T(1024)S(1)}, f32[768]{0:T(1024)}, u32[]{:S(2)}) copy-start(f32[768]{0:T(1024)} %param.26) | copy-start | bytes 9220
  551.2 10.5 %copy-start.24 = (f32[2,384]{1,0:T(2,128)S(1)}, f32[2,384]{1,0:T(2,128)}, u32[]{:S(2)}) copy-start(f32[2,384]{1,0:T(2,128)} %copy-done.23) | copy-start | bytes 9220
  551.2 10.5 %copy-start.26 = (f32[768]{0:T(1024)S(1)}, f32[768]{0:T(1024)}, u32[]{:S(2)}) copy-start(f32[768]{0:T(1024)} %param.27) | copy-start | bytes 9220
  551.2 10.5 %copy-start.28 = (f32[2,384]{1,0:T(2,128)S(1)}, f32[2,384]{1,0:T(2,128)}, u32[]{:S(2)}) copy-start(f32[2,384]{1,0:T(2,128)} %copy-done.27) | copy-start | bytes 9220
  551.2 10.5 %copy-start.31 = (f32[768]{0:T(1024)S(1)}, f32[768]{0:T(1024)}, u32[]{:S(2)}) copy-start(f32[768]{0:T(1024)} %param.28) | copy-start | bytes 9220
  571.0 0.7 copy-start.49
  571.7 8.8 copy-start.19
  580.5 92.9 %copy-start.33 = (f32[2,384]{1,0:T(2,128)S(1)}, f32[2,384]{1,0:T(2,128)}, u32[]{:S(2)}) copy-start(f32[2,384]{1,0:T(2,128)} %copy-done.32) | copy-start | bytes 9220
  580.5 92.9 %copy-start.34 = (f32[768]{0:T(1024)S(1)}, f32[768]{0:T(1024)}, u32[]{:S(2)}) copy-start(f32[768]{0:T(1024)} %param.21) | copy-start | bytes 9220
  580.5 95.1 %copy-start.42 = (f32[2,384]{1,0:T(2,128)S(1)}, f32[2,384]{1,0:T(2,128)}, u32[]{:S(2)}) copy-start(f32[2,384]{1,0:T(2,128)} %copy-done.41) | copy-start | bytes 9220
  580.5 95.1 %copy-start.38 = (f32[2,384]{1,0:T(2,128)S(1)}, f32[2,384]{1,0:T(2,128)}, u32[]{:S(2)}) copy-start(f32[2,384]{1,0:T(2,128)} %copy-done.37) | copy-start | bytes 9220
  580.9 97.5 %copy-start.36 = (f32[2,384]{1,0:T(2,128)S(1)}, f32[2,384]{1,0:T(2,128)}, u32[]{:S(2)}) copy-start(f32[2,384]{1,0:T(2,128)} %copy-done.35) | copy-start | bytes 9220
  580.9 97.5 %copy-start.40 = (f32[2,384]{1,0:T(2,128)S(1)}, f32[2,384]{1,0:T(2,128)}, u32[]{:S(2)}) copy-start(f32[2,384]{1,0:T(2,128)} %copy-done.39) | copy-start | bytes 9220
  673.3 5.1 copy-start.10
  673.3 5.1 copy-start.11
  673.3 5.1 copy-start.16
  678.3 3.1 copy-start.43
  678.3 3.1 copy-start.44
  678.3 3.1 copy-start.46
  678.4 3.1 copy-start.47
  986.5 8.8 slice-start
  986.5 8.8 slice-start.1
  986.5 8.8 slice-start.2
  (2 other events, 1.2 us)
Sparse Core Ops, SparseCore 0:
  14.7 40.1 all-gather.2
  126.0 47.8 reduce-scatter.2
  235.8 37.4 all-gather.4
  543.5 80.2 all-reduce.7
  626.2 47.1 reduce-scatter.4
  681.3 305.1 all-reduce.5
where the time goes:
time: 1010 us
  waiting for transfers between devices  454 us (45%)
  matrix products  354 us (35%)
  other arithmetic  75.9 us (8%)
  blocking collectives  64 us (6%)
  local copies, waits for them, and re-layouts  40.5 us (4%)
  between operations  14.8 us (1%)
    psum x1, waiting for transfers between devices, body(): lax.psum((grad_gain_one, grad_shift_one, grad_b_out, grad_gain_two, grad_...  263 us
    dot_general x6, matrix products, row_backward(): jnp.einsum('hqk,khe->qhe', score_grad, key_rows, preferred_element_type=j...  89.1 us
    dot_general x6, matrix products, row_backward(): jnp.einsum('hqk,qhe->khe', score_grad, query_block, preferred_element_typ...  87.3 us
    reduce_scatter x1, waiting for transfers between devices, body(): lax.psum_scatter(partial_out.astype(jnp.bfloat16), ('th', 'tw'), scatter_...  47.9 us
    reduce_scatter x1, waiting for transfers between devices, body(): lax.psum_scatter(grad_normed.astype(jnp.bfloat16), ('th', 'tw'), scatter_...  45.2 us
    psum x1, blocking collectives, body(): lax.psum((grad_gain_one, grad_shift_one, grad_b_out, grad_gain_two, grad_...  42.5 us
    all_gather x1, waiting for transfers between devices, body(): gathered = lax.all_gather(normed_low, ('th', 'tw'), axis=1, tiled=True)  40.1 us
    all_gather x1, waiting for transfers between devices, body(): grad_whole = lax.all_gather(grad_branch, ('th', 'tw'), axis=1, tiled=True)  37.6 us
  transfers between devices with their start and end apart: 6, of which 6 were waited for; matrix products, arithmetic and copies ran while one was open for 5% of the time, Pallas kernels for 0%

commit v1 on v0

--- a/solution.py
+++ b/solution.py
@@ -116,7 +116,24 @@
     inputs = tokens.astype(jnp.float32)
     normed_one, norm_one_back = jax.vjp(layer_norm, inputs, norm1_gain, norm1_shift)
     normed_low = normed_one.astype(jnp.bfloat16)
-    gathered = lax.all_gather(normed_low, ("th", "tw"), axis=1, tiled=True)
+    prior, step_out, a_now = (
+        lax.axis_size(("th", "tw")),
+        lax.axis_index(("th", "tw")),
+        normed_low.shape[1],
+    )
+    left_arr, tile_out = (normed_low, 1)
+    while tile_out < prior:
+        left_arr = jnp.concatenate(
+            [
+                left_arr,
+                lax.ppermute(
+                    left_arr, ("th", "tw"), [(c, (c - tile_out) % prior) for c in range(prior)]
+                ),
+            ],
+            axis=1,
+        )
+        tile_out = 2 * tile_out
+    gathered = jnp.roll(left_arr, shift=step_out * a_now, axis=1)
     bias_rows = jnp.stack([b_qv[0], jnp.zeros_like(b_qv[0]), b_qv[1]])
     projected = jnp.einsum("rld,cde->rcle", gathered, w_qkv, preferred_element_type=jnp.float32)
     projected_low = (projected + bias_rows[None, :, None, :]).astype(jnp.bfloat16)

time: 1010 us -> 1010 us (level)
    all_gather x1 -> x0, waiting for transfers between devices: 40.1 us -> none  [body(): gathered = lax.all_gather(normed_low, ('th', 'tw'), axis=1, tiled=True)]
    ppermute x0 -> x2, waiting for transfers between devices: none -> 30.1 us  [body(): lax.ppermute(left_arr, ('th', 'tw'), [(c, (c - tile_out) % prior) for c i...]
    unnamed x94 -> x102, local copies, waits for them, and re-layouts: 14.5 us -> 20.4 us
  transfers between devices with their start and end apart: 6 -> 7, of which waited for: 6 -> 7; matrix products, arithmetic and copies ran while one was open for 5% -> 5% of each run, Pallas kernels for 0% -> 0%
where the time goes in v1:
time: 1010 us
  waiting for transfers between devices  446 us (44%)
  matrix products  352 us (35%)
  other arithmetic  77.6 us (8%)
  blocking collectives  64 us (6%)
  local copies, waits for them, and re-layouts  49.7 us (5%)
  between operations  14.5 us (1%)
    psum x1, waiting for transfers between devices, body(): lax.psum((grad_gain_one, grad_shift_one, grad_b_out, grad_gain_two, grad_...  263 us
    dot_general x6, matrix products, row_backward(): jnp.einsum('hqk,khe->qhe', score_grad, key_rows, preferred_element_type=j...  88.3 us
    dot_general x6, matrix products, row_backward(): jnp.einsum('hqk,qhe->khe', score_grad, query_block, preferred_element_typ...  86.7 us
    reduce_scatter x1, waiting for transfers between devices, body(): lax.psum_scatter(partial_out.astype(jnp.bfloat16), ('th', 'tw'), scatter_...  50 us
    reduce_scatter x1, waiting for transfers between devices, body(): lax.psum_scatter(grad_normed.astype(jnp.bfloat16), ('th', 'tw'), scatter_...  45.2 us
    psum x1, blocking collectives, body(): lax.psum((grad_gain_one, grad_shift_one, grad_b_out, grad_gain_two, grad_...  42.5 us
    all_gather x1, waiting for transfers between devices, body(): grad_whole = lax.all_gather(grad_branch, ('th', 'tw'), axis=1, tiled=True)  37.6 us
    dot_general x6, matrix products, row_backward(): jnp.einsum('qhe,khe->hqk', upstream, value_rows, preferred_element_type=j...  30.9 us
  transfers between devices with their start and end apart: 7, of which 7 were waited for; matrix products, arithmetic and copies ran while one was open for 5% of the time, Pallas kernels for 0%

profile of v1, /device:TPU:0, one launch (start us, length us, event | category | flops | bytes accessed | tf_op | source)
XLA Modules:
  0.0 1008.1 jit_solution(17914892453834384539)
XLA Ops:
  11.2 2.8 constant_dynamic-update-slice_fusion.5
  16.4 26.5 %collective-permute-done = bf16[2,384,768]{2,1,0:T(8,128)(2,1)S(1)} collective-permute-done((bf16[2,384,768]{2,1,0:T(8,128)(2,1)S(1)}, bf16[2,384,768]{2,1,0:T(8,128)(2,1)S(1)}, u32[]{:S(2)}, u32[]{:S(2)}) %collective-permute-start) | collective-permute-done | bytes 1179680 | tf_op jit(solution)/shard_map/ppermute | solution.py:129
  45.7 3.6 collective-permute-done.1
  49.4 3.2 constant_dynamic-update-slice_fusion.3
  54.8 3.2 constant_dynamic-update-slice_fusion
  58.0 6.9 fusion.156
  64.9 59.3 %while.22 = (s32[]{:T(128)}, bf16[2,1536,192]{1,2,0:T(8,128)(2,1)S(1)}, f32[2,3,1536]{2,1,0:T(4,128)S(1)}, bf16[2,3,1536,192]{2,3,1,0:T(8,128)(2,1)}, s32[2,1536...) while((s32[]{:T(128)}, bf16[2,1536,192]{1,2,0:T(8,128)(2,1)S(1)}, ...), condition=%wide.region_9.10_spmd, body=%wide.region_2.9_spmd.sunk | while | flops 1901302272 | bytes 107581632 | solution.py:140
  71.7 2.8 fusion.325
  74.5 3.5 fusion.326
  82.0 5.2 fusion.329
  87.2 3.5 fusion.331
  90.7 3.5 fusion.330
  100.9 2.8 fusion.325
  103.7 3.5 fusion.326
  111.3 5.2 fusion.329
  116.4 3.5 fusion.331
  120.0 3.5 fusion.330
  124.2 4.9 convolution_convert_fusion
  129.2 50.0 %reduce-scatter.3.cloned.1.call-done = bf16[2,384,768]{2,1,0:T(8,128)(2,1)} async-done(((bf16[2,1536,768]{2,1,0:T(8,128)(2,1)}), bf16[2,384,768]{2,1,0:T(8,128)(2,1)}) %reduce-scatter.3.cloned.1.call-update) | async-done | bytes 1179664 | tf_op jit(solution)/shard_map/reduce_scatter | solution.py:143
  183.0 9.2 fusion.167
  192.2 23.5 %multiply_convert_fusion.3 = (bf16[2,384,3072]{2,1,0:T(8,128)(2,1)}, f32[2,384,3072]{2,1,0:T(8,128)}) fusion(f32[2,384,3072]{2,1,0:T(8,128)S(1)} %get-tuple-element.166, f32[3072]{0:T(1024)S(1)} %copy-done.46, u8[384,3072]{1,0:T(8,128)(4,1)S(1)} %get-tuple-element.78, u8[384,3072]{1,0:T(8,128)(4,1)S(1)} %get-tuple-element.77), kind=kLoop, calls=%fused_computation.126 | loop fusion | flops 167510016 | bytes 25964544 | tf_op jit(solution)/shard_map/convert_element_type | solution.py:155
  215.7 12.5 %convert_reduce_fusion = (f32[3072]{0:T(1024)}, bf16[2,384,3072]{2,1,0:T(8,128)(2,1)}) fusion(f32[2,384,3072]{2,1,0:T(8,128)} %get-tuple-element.123, bf16[2,384,768]{2,1,0:T(8,128)(2,1)S(1)} %copy-done.15, bf16[3072,768]{1,0:T(8,128)(2,1)} %param.31, f32[2,384,3072]{2,1,0:T(8,128)S(1)} %get-tuple-element.166, f32[3072]{0:T(1024)S(1)} %copy-done.46), kind=kOutput, calls=%fused_computation.124 | convolution fusion | flops 3663983616 | bytes 29515776 | tf_op jit(solution)/shard_map/rld,fd->rlf/dot_general | solution.py:164
  228.2 8.1 fusion.189
  238.3 2.7 convert_reduce_fusion.4
  241.1 37.6 %all-gather.2.cloned.1.call-done = bf16[2,1536,768]{2,1,0:T(8,128)(2,1)} async-done(((bf16[2,384,768]{2,1,0:T(8,128)(2,1)}), bf16[2,1536,768]{2,1,0:T(8,128)(2,1)}) %all-gather.2.cloned.1.call-update) | async-done | bytes 4718608 | tf_op jit(solution)/shard_map/all_gather | solution.py:177
  278.7 5.0 convolution_convert_fusion.1
  283.7 252.7 %while.23 = (s32[]{:T(128)}, bf16[2,3,1536,192]{2,3,1,0:T(8,128)(2,1)}, bf16[2,3,1536,192]{2,3,1,0:T(8,128)(2,1)}, s32[2,1536]{1,0:T(2,128)S(1)}, f32[2,3,1536]{...) while((s32[]{:T(128)}, ...), condition=%wide.region_19.20_spmd, body=%wide.region_15.19_spmd.sunk | while | flops 4682926080 | bytes 364640672 | solution.py:184
  292.0 2.6 copy-done.2
  299.6 4.3 copy-done.3
  305.8 5.1 fusion.376
  310.9 15.2 %fusion.382 = bf16[3,64,512]{2,1,0:T(8,128)(2,1)} fusion(bf16[1536,3,64]{0,2,1:T(8,128)(2,1)S(1)} %bitcast.312, f32[3,512,1536]{2,1,0:T(8,128)} %copy-done.4, f32[3,512,1536]{2,1,0:T(8,128)} %fusion.376), kind=kOutput, calls=%fused_computation.94.clone.1 | convolution fusion | flops 320965632 | bytes 19660800 | tf_op jit(solution)/shard_map/while/body/eval_jaxpr/hqk,khe->qhe/dot_general | solution.py:82
  326.1 15.3 %fusion.377 = f32[3,64,1536]{2,1,0:T(8,128)} fusion(bf16[512,3,64]{0,2,1:T(8,128)(2,1)} %bitcast.323, f32[3,512,1536]{2,1,0:T(8,128)} %copy-done.4, f32[3,512,1536]{2,1,0:T(8,128)} %fusion.376), kind=kOutput, calls=%fused_computation.63.clone.1 | convolution fusion | flops 320867328 | bytes 20250624 | tf_op jit(solution)/shard_map/while/body/eval_jaxpr/hqk,qhe->khe/dot_general | solution.py:86
  341.5 5.1 fusion.380
  346.6 14.2 %fusion.384 = bf16[3,64,512]{2,1,0:T(8,128)(2,1)S(1)} fusion(bf16[1536,3,64]{0,2,1:T(8,128)(2,1)S(1)} %bitcast.313, f32[3,512,1536]{2,1,0:T(8,128)} %copy-done.3, f32[3,512,1536]{2,1,0:T(8,128)} %fusion.380), kind=kOutput, calls=%fused_computation.92.clone.1 | convolution fusion | flops 320965632 | bytes 19660800 | tf_op jit(solution)/shard_map/while/body/eval_jaxpr/hqk,khe->qhe/dot_general | solution.py:82
  360.8 5.2 fusion.378
  366.0 14.8 %fusion.383 = bf16[3,64,512]{2,1,0:T(8,128)(2,1)} fusion(bf16[1536,3,64]{0,2,1:T(8,128)(2,1)S(1)} %bitcast.314, f32[3,512,1536]{2,1,0:T(8,128)} %copy-done.2, f32[3,512,1536]{2,1,0:T(8,128)} %fusion.378), kind=kOutput, calls=%fused_computation.93.clone.1 | convolution fusion | flops 320965632 | bytes 19660800 | tf_op jit(solution)/shard_map/while/body/eval_jaxpr/hqk,khe->qhe/dot_general | solution.py:82
  380.8 14.1 %fusion.379 = f32[3,64,1536]{2,1,0:T(8,128)} fusion(bf16[512,3,64]{0,2,1:T(8,128)(2,1)S(1)} %bitcast.321, f32[3,512,1536]{2,1,0:T(8,128)} %copy-done.2, f32[3,512,1536]{2,1,0:T(8,128)} %fusion.378), kind=kOutput, calls=%fused_computation.67.clone.1 | convolution fusion | flops 320867328 | bytes 20250624 | tf_op jit(solution)/shard_map/while/body/eval_jaxpr/hqk,qhe->khe/dot_general | solution.py:86
  394.8 13.9 %fusion.381 = bf16[3,64,1536]{2,1,0:T(8,128)(2,1)S(1)} fusion(f32[3,64,1536]{2,1,0:T(8,128)} %fusion.377, f32[3,64,1536]{2,1,0:T(8,128)} %fusion.379, bf16[512,3,64]{0,2,1:T(8,128)(2,1)S(1)} %bitcast.319, f32[3,512,1536]{2,1,0:T(8,128)} %copy-done.3, f32[3,512,1536]{2,1,0:T(8,128)} %fusion.380), kind=kOutput, calls=%fused_computation.79.clone.1 | convolution fusion | flops 321752064 | bytes 22020096 | tf_op jit(solution)/shard_map/while/body/eval_jaxpr/hqk,qhe->khe/dot_general | solution.py:86
  418.1 2.6 copy-done.2
  425.7 4.3 copy-done.3
  431.9 5.1 fusion.376
  437.0 15.2 %fusion.382 = bf16[3,64,512]{2,1,0:T(8,128)(2,1)} fusion(bf16[1536,3,64]{0,2,1:T(8,128)(2,1)S(1)} %bitcast.312, f32[3,512,1536]{2,1,0:T(8,128)} %copy-done.4, f32[3,512,1536]{2,1,0:T(8,128)} %fusion.376), kind=kOutput, calls=%fused_computation.94.clone.1 | convolution fusion | flops 320965632 | bytes 19660800 | tf_op jit(solution)/shard_map/while/body/eval_jaxpr/hqk,khe->qhe/dot_general | solution.py:82
  452.2 15.3 %fusion.377 = f32[3,64,1536]{2,1,0:T(8,128)} fusion(bf16[512,3,64]{0,2,1:T(8,128)(2,1)} %bitcast.323, f32[3,512,1536]{2,1,0:T(8,128)} %copy-done.4, f32[3,512,1536]{2,1,0:T(8,128)} %fusion.376), kind=kOutput, calls=%fused_computation.63.clone.1 | convolution fusion | flops 320867328 | bytes 20250624 | tf_op jit(solution)/shard_map/while/body/eval_jaxpr/hqk,qhe->khe/dot_general | solution.py:86
  467.6 5.1 fusion.380
  472.7 14.2 %fusion.384 = bf16[3,64,512]{2,1,0:T(8,128)(2,1)S(1)} fusion(bf16[1536,3,64]{0,2,1:T(8,128)(2,1)S(1)} %bitcast.313, f32[3,512,1536]{2,1,0:T(8,128)} %copy-done.3, f32[3,512,1536]{2,1,0:T(8,128)} %fusion.380), kind=kOutput, calls=%fused_computation.92.clone.1 | convolution fusion | flops 320965632 | bytes 19660800 | tf_op jit(solution)/shard_map/while/body/eval_jaxpr/hqk,khe->qhe/dot_general | solution.py:82
  486.9 5.2 fusion.378
  492.1 14.8 %fusion.383 = bf16[3,64,512]{2,1,0:T(8,128)(2,1)} fusion(bf16[1536,3,64]{0,2,1:T(8,128)(2,1)S(1)} %bitcast.314, f32[3,512,1536]{2,1,0:T(8,128)} %copy-done.2, f32[3,512,1536]{2,1,0:T(8,128)} %fusion.378), kind=kOutput, calls=%fused_computation.93.clone.1 | convolution fusion | flops 320965632 | bytes 19660800 | tf_op jit(solution)/shard_map/while/body/eval_jaxpr/hqk,khe->qhe/dot_general | solution.py:82
  506.9 14.1 %fusion.379 = f32[3,64,1536]{2,1,0:T(8,128)} fusion(bf16[512,3,64]{0,2,1:T(8,128)(2,1)S(1)} %bitcast.321, f32[3,512,1536]{2,1,0:T(8,128)} %copy-done.2, f32[3,512,1536]{2,1,0:T(8,128)} %fusion.378), kind=kOutput, calls=%fused_computation.67.clone.1 | convolution fusion | flops 320867328 | bytes 20250624 | tf_op jit(solution)/shard_map/while/body/eval_jaxpr/hqk,qhe->khe/dot_general | solution.py:86
  520.9 13.9 %fusion.381 = bf16[3,64,1536]{2,1,0:T(8,128)(2,1)S(1)} fusion(f32[3,64,1536]{2,1,0:T(8,128)} %fusion.377, f32[3,64,1536]{2,1,0:T(8,128)} %fusion.379, bf16[512,3,64]{0,2,1:T(8,128)(2,1)S(1)} %bitcast.319, f32[3,512,1536]{2,1,0:T(8,128)} %copy-done.3, f32[3,512,1536]{2,1,0:T(8,128)} %fusion.380), kind=kOutput, calls=%fused_computation.79.clone.1 | convolution fusion | flops 321752064 | bytes 22020096 | tf_op jit(solution)/shard_map/while/body/eval_jaxpr/hqk,qhe->khe/dot_general | solution.py:86
  536.5 7.4 fusion.176
  545.8 7.7 bitcast_convert_fusion
  553.6 10.5 %convolution_bitcast_fusion = f32[3072,768]{1,0:T(8,128)} fusion(bf16[2,384,3072]{2,1,0:T(8,128)(2,1)} %get-tuple-element.122, bf16[2,384,768]{2,1,0:T(8,128)(2,1)} %param.33), kind=kOutput, calls=%fused_computation.140 | convolution fusion | flops 3623878656 | bytes 15335424 | tf_op jit(solution)/shard_map/rlf,rld->fd/dot_general | solution.py:160
  564.1 9.2 convolution_bitcast_fusion.1
  574.0 8.8 add_convert_fusion.3
  583.3 21.5 %psum.87 = bf16[2,192]{1,0:T(2,128)(2,1)S(1)} all-reduce(bf16[2,192]{1,0:T(2,128)(2,1)S(1)} %slice_reduce_fusion), channel_id=1, replica_groups=mesh['dp'=8,'th'=2,'tw'=2] {'dp'}, use_global_device_ids=true, to_apply=%region_29.30 | all-reduce | flops 384 | bytes 1536 | tf_op jit(solution)/shard_map/psum | solution.py:195
  605.3 20.9 %all-reduce.8.cloned.1.call-done = (bf16[3,768,192]{1,2,0:T(8,128)(2,1)}, bf16[192,768]{1,0:T(8,128)(2,1)}) async-done(((bf16[3,768,192]{1,2,0:T(8,128)(2,1)}, bf16[192,768]{1,0:T(8,128)(2,1)}), (bf16[3,768,192]{1,2,0:T(8,128)(2,1)}, bf16[192,768]{1,0:T(8,128)(2,1)})) %all-reduce.8.cloned.1.call-update) | async-done | bytes 1179664 | tf_op jit(solution)/shard_map/psum | solution.py:194
  628.0 2.5 convert_element_type.154
  630.5 45.2 %reduce-scatter.5.cloned.1.call-done = bf16[2,384,768]{2,1,0:T(8,128)(2,1)} async-done(((bf16[2,1536,768]{2,1,0:T(8,128)(2,1)}), bf16[2,384,768]{2,1,0:T(8,128)(2,1)}) %reduce-scatter.5.cloned.1.call-update) | async-done | bytes 1179664 | tf_op jit(solution)/shard_map/reduce_scatter | solution.py:188
  678.0 2.7 fusion.165
  680.8 3.0 convert_reduce_fusion.3
  683.8 42.5 %all-reduce = (f32[768]{0:T(1024)}, f32[768]{0:T(1024)}, f32[768]{0:T(1024)}, f32[768]{0:T(1024)}, f32[768]{0:T(1024)}, /*index=5*/f32[3072]{0:T(1024)}, f32[768]{0:T(1024)}) all-reduce(f32[768]{0:T(1024)S(1)} %get-tuple-element.81, f32[768]{0:T(1024)S(1)} %get-tuple-element.85, ...), channel_id=1, replica_groups=mesh['dp'=8,'th'=2,'tw'=2] {'dp','th','tw'}, use_global_device_ids=true, to_apply=%region_24.25 | all-reduce | flops 7680 | bytes 61440 | tf_op jit(solution)/shard_map/psum | solution.py:198
  726.3 262.5 %all-reduce.6.cloned.1.call-done = (f32[768,3072]{1,0:T(8,128)}, f32[3072,768]{1,0:T(8,128)}) async-done(((f32[768,3072]{1,0:T(8,128)}, f32[3072,768]{1,0:T(8,128)}), (f32[768,3072]{1,0:T(8,128)}, f32[3072,768]{1,0:T(8,128)})) %all-reduce.6.cloned.1.call-update) | async-done | bytes 18874384 | tf_op jit(solution)/shard_map/psum | solution.py:198
  988.8 8.8 copy.64
  997.6 3.7 copy.65
  (223 shorter events, 78.3 us)
Async XLA Ops:
  7.2 50.8 %copy-start = (bf16[3,768,192]{1,2,0:T(8,128)(2,1)S(1)}, bf16[3,768,192]{1,2,0:T(8,128)(2,1)}, u32[]{:S(2)}) copy-start(bf16[3,768,192]{1,2,0:T(8,128)(2,1)} %param.23) | copy-start | bytes 2654212
  7.2 172.0 %reduce-scatter.3.cloned.1.call-start = ((), (), s32[]{:S(2)}) async-start(), calls=%async_computation.2 | async-start | bytes 5898240 | tf_op jit(solution)/shard_map/reduce_scatter | solution.py:143
  8.8 5.2 copy-start.33
  8.8 35.7 %copy-start.49 = (f32[2,192]{1,0:T(2,128)S(1)}, f32[2,192]{1,0:T(2,128)}, u32[]{:S(2)}) copy-start(f32[2,192]{1,0:T(2,128)} %param.24) | copy-start | bytes 4612
  11.2 5.2 copy-start.38
  14.0 28.9 %collective-permute-start = (bf16[2,384,768]{2,1,0:T(8,128)(2,1)S(1)}, bf16[2,384,768]{2,1,0:T(8,128)(2,1)S(1)}, u32[]{:S(2)}, u32[]{:S(2)}) collective-permute-start(bf16[2,384,768]{2,1,0:T(8,128)(2,1)S(1)} %get-tuple-element.125), channel_id=1, source_target_pairs={{0,3},{1,0},{2,1},{3,2},{4,7},{5,4},{6,5},{7,6},{8,11},{9,8},{10,9... | collective-permute-start | bytes 3538952 | tf_op jit(solution)/shard_map/ppermute | solution.py:129
  44.5 4.9 collective-permute-start.1
  58.0 6.9 copy-start.17
  58.0 6.9 copy-start.21
  124.2 5.0 copy-start.18
  124.2 55.0 %copy-start.5 = (bf16[2,384,768]{2,1,0:T(8,128)(2,1)S(1)}, bf16[2,384,768]{2,1,0:T(8,128)(2,1)}, u32[]{:S(2)}) copy-start(bf16[2,384,768]{2,1,0:T(8,128)(2,1)} %param.19) | copy-start | bytes 3538948
  124.2 55.0 %copy-start.22 = (f32[768]{0:T(1024)S(1)}, f32[768]{0:T(1024)}, u32[]{:S(2)}) copy-start(f32[768]{0:T(1024)} %param.26) | copy-start | bytes 9220
  129.1 53.8 %copy-start.26 = (f32[768]{0:T(1024)S(1)}, f32[768]{0:T(1024)}, u32[]{:S(2)}) copy-start(f32[768]{0:T(1024)} %param.27) | copy-start | bytes 9220
  129.1 53.8 %copy-start.31 = (f32[768]{0:T(1024)S(1)}, f32[768]{0:T(1024)}, u32[]{:S(2)}) copy-start(f32[768]{0:T(1024)} %param.28) | copy-start | bytes 9220
  129.1 53.8 %copy-start.46 = (f32[3072]{0:T(1024)S(1)}, f32[3072]{0:T(1024)}, u32[]{:S(2)}) copy-start(f32[3072]{0:T(1024)} %param.30) | copy-start | bytes 36868
  129.2 149.5 %all-gather.2.cloned.1.call-start = ((), (), s32[]{:S(2)}) async-start(), calls=%async_computation.3 | async-start | bytes 5898240 | tf_op jit(solution)/shard_map/all_gather | solution.py:177
  179.2 3.8 copy-start.7
  181.0 57.3 %copy-start.24 = (f32[2,384]{1,0:T(2,128)}, f32[2,384]{1,0:T(2,128)S(1)}, u32[]{:S(2)}) copy-start(f32[2,384]{1,0:T(2,128)S(1)} %broadcast_multiply_fusion) | copy-start | bytes 9220
  183.0 55.3 %copy-start.28 = (f32[2,384]{1,0:T(2,128)}, f32[2,384]{1,0:T(2,128)S(1)}, u32[]{:S(2)}) copy-start(f32[2,384]{1,0:T(2,128)S(1)} %fusion.185) | copy-start | bytes 9220
  192.2 23.5 %copy-start.15 = (bf16[2,384,768]{2,1,0:T(8,128)(2,1)S(1)}, bf16[2,384,768]{2,1,0:T(8,128)(2,1)}, u32[]{:S(2)}) copy-start(bf16[2,384,768]{2,1,0:T(8,128)(2,1)} %param.33) | copy-start | bytes 3538948
  236.3 4.8 copy-start.9
  236.3 4.8 copy-start.36
  238.3 40.4 %copy-start.30 = (bf16[192,768]{1,0:T(8,128)(2,1)S(1)}, bf16[192,768]{1,0:T(8,128)(2,1)}, u32[]{:S(2)}) copy-start(bf16[192,768]{1,0:T(8,128)(2,1)} %param.25) | copy-start | bytes 884740
  238.3 45.4 %copy-start.40 = (f32[2,384]{1,0:T(2,128)}, f32[2,384]{1,0:T(2,128)S(1)}, u32[]{:S(2)}) copy-start(f32[2,384]{1,0:T(2,128)S(1)} %negate_multiply_fusion.2) | copy-start | bytes 9220
  241.1 385.1 %all-reduce.8.cloned.1.call-start = ((), (), s32[]{:S(2)}) async-start(), calls=%async_computation.6 | async-start | bytes 2359296 | tf_op jit(solution)/shard_map/psum | solution.py:194
  287.1 4.9 copy-start.12
  291.0 3.6 copy-start.2
  297.1 7.7 copy-start.4
  299.6 4.3 copy-start.3
  394.8 14.0 %copy-start.13 = (bf16[3,64,512]{2,1,0:T(8,128)(2,1)S(1)}, bf16[3,64,512]{2,1,0:T(8,128)(2,1)}, u32[]{:S(2)}) copy-start(bf16[3,64,512]{2,1,0:T(8,128)(2,1)} %fusion.382) | copy-start | bytes 589828 | tf_op jit(solution)/shard_map/while
  394.8 14.0 %copy-start.14 = (bf16[3,64,512]{2,1,0:T(8,128)(2,1)S(1)}, bf16[3,64,512]{2,1,0:T(8,128)(2,1)}, u32[]{:S(2)}) copy-start(bf16[3,64,512]{2,1,0:T(8,128)(2,1)} %fusion.383) | copy-start | bytes 589828 | tf_op jit(solution)/shard_map/while
  413.2 4.9 copy-start.12
  417.1 3.6 copy-start.2
  423.2 7.7 copy-start.4
  425.7 4.3 copy-start.3
  520.9 14.0 %copy-start.13 = (bf16[3,64,512]{2,1,0:T(8,128)(2,1)S(1)}, bf16[3,64,512]{2,1,0:T(8,128)(2,1)}, u32[]{:S(2)}) copy-start(bf16[3,64,512]{2,1,0:T(8,128)(2,1)} %fusion.382) | copy-start | bytes 589828 | tf_op jit(solution)/shard_map/while
  520.9 14.0 %copy-start.14 = (bf16[3,64,512]{2,1,0:T(8,128)(2,1)S(1)}, bf16[3,64,512]{2,1,0:T(8,128)(2,1)}, u32[]{:S(2)}) copy-start(bf16[3,64,512]{2,1,0:T(8,128)(2,1)} %fusion.383) | copy-start | bytes 589828 | tf_op jit(solution)/shard_map/while
  536.5 7.4 copy-start.19
  536.5 7.4 copy-start.50
  545.7 130.0 %reduce-scatter.5.cloned.1.call-start = ((), (), s32[]{:S(2)}) async-start(), calls=%async_computation.4 | async-start | bytes 5898240 | tf_op jit(solution)/shard_map/reduce_scatter | solution.py:188
  553.4 435.4 %all-reduce.6.cloned.1.call-start = ((), (), s32[]{:S(2)}) async-start(), calls=%async_computation.5 | async-start | bytes 37748736 | tf_op jit(solution)/shard_map/psum | solution.py:198
  553.5 10.6 %copy-start.6 = (bf16[2,384,768]{2,1,0:T(8,128)(2,1)S(1)}, bf16[2,384,768]{2,1,0:T(8,128)(2,1)}, u32[]{:S(2)}) copy-start(bf16[2,384,768]{2,1,0:T(8,128)(2,1)} %param.19) | copy-start | bytes 3538948
  553.5 10.6 %copy-start.8 = (bf16[2,384,768]{2,1,0:T(8,128)(2,1)S(1)}, bf16[2,384,768]{2,1,0:T(8,128)(2,1)}, u32[]{:S(2)}) copy-start(bf16[2,384,768]{2,1,0:T(8,128)(2,1)} %reduce-scatter.3.cloned.1.call-done) | copy-start | bytes 3538948
  553.5 10.5 %copy-start.23 = (f32[768]{0:T(1024)S(1)}, f32[768]{0:T(1024)}, u32[]{:S(2)}) copy-start(f32[768]{0:T(1024)} %param.26) | copy-start | bytes 9220
  553.5 10.5 %copy-start.25 = (f32[2,384]{1,0:T(2,128)S(1)}, f32[2,384]{1,0:T(2,128)}, u32[]{:S(2)}) copy-start(f32[2,384]{1,0:T(2,128)} %copy-done.24) | copy-start | bytes 9220
  553.5 10.5 %copy-start.27 = (f32[768]{0:T(1024)S(1)}, f32[768]{0:T(1024)}, u32[]{:S(2)}) copy-start(f32[768]{0:T(1024)} %param.27) | copy-start | bytes 9220
  553.6 10.5 %copy-start.29 = (f32[2,384]{1,0:T(2,128)S(1)}, f32[2,384]{1,0:T(2,128)}, u32[]{:S(2)}) copy-start(f32[2,384]{1,0:T(2,128)} %copy-done.28) | copy-start | bytes 9220
  553.6 10.5 %copy-start.32 = (f32[768]{0:T(1024)S(1)}, f32[768]{0:T(1024)}, u32[]{:S(2)}) copy-start(f32[768]{0:T(1024)} %param.28) | copy-start | bytes 9220
  574.0 8.8 copy-start.20
  582.8 92.9 %copy-start.34 = (f32[2,384]{1,0:T(2,128)S(1)}, f32[2,384]{1,0:T(2,128)}, u32[]{:S(2)}) copy-start(f32[2,384]{1,0:T(2,128)} %copy-done.33) | copy-start | bytes 9220
  582.8 92.9 %copy-start.35 = (f32[768]{0:T(1024)S(1)}, f32[768]{0:T(1024)}, u32[]{:S(2)}) copy-start(f32[768]{0:T(1024)} %param.21) | copy-start | bytes 9220
  582.8 95.1 %copy-start.43 = (f32[2,384]{1,0:T(2,128)S(1)}, f32[2,384]{1,0:T(2,128)}, u32[]{:S(2)}) copy-start(f32[2,384]{1,0:T(2,128)} %copy-done.42) | copy-start | bytes 9220
  582.8 95.2 %copy-start.39 = (f32[2,384]{1,0:T(2,128)S(1)}, f32[2,384]{1,0:T(2,128)}, u32[]{:S(2)}) copy-start(f32[2,384]{1,0:T(2,128)} %copy-done.38) | copy-start | bytes 9220
  583.2 97.5 %copy-start.37 = (f32[2,384]{1,0:T(2,128)S(1)}, f32[2,384]{1,0:T(2,128)}, u32[]{:S(2)}) copy-start(f32[2,384]{1,0:T(2,128)} %copy-done.36) | copy-start | bytes 9220
  583.3 97.5 %copy-start.41 = (f32[2,384]{1,0:T(2,128)S(1)}, f32[2,384]{1,0:T(2,128)}, u32[]{:S(2)}) copy-start(f32[2,384]{1,0:T(2,128)} %copy-done.40) | copy-start | bytes 9220
  675.7 5.1 copy-start.10
  675.7 5.1 copy-start.11
  675.7 5.1 copy-start.16
  680.7 3.1 copy-start.44
  680.7 3.1 copy-start.45
  680.7 3.1 copy-start.47
  988.8 8.8 slice-start
  988.8 8.8 slice-start.1
  988.8 8.8 slice-start.2
  (5 other events, 10.0 us)
Sparse Core Ops, SparseCore 0:
  129.3 49.8 reduce-scatter.2
  241.2 37.4 all-gather.1
  545.8 80.2 all-reduce.7
  628.5 47.1 reduce-scatter.4
  683.7 305.1 all-reduce.5
